TPU v7x, 128 devices: a whole 4x4x4 slice. The times are simulated.
128 devices in a mesh: group: 8 (over z, core), member: 16 (over x, y).
Axes of the slice: x: 4, y: 4, z: 4, core: 2. Of those that a mesh axis runs over, the one named last changes fastest.
Arguments:
- hidden: bfloat16 [12288, 2048], P('group'), may hold values from -6 to 6
- token_slab: int32 [12288, 1], P(('group', 'member')), may hold values from 0 to 127; in each aligned block of 96 rows (0 to 95, 96 to 191, ...) at most 2 rows name the same one
- token_row: int32 [12288], P(('group', 'member')), may hold values from 0 to 2047
- slab_owner: int32 [128], replicated, may hold values from 0 to 127, each once
- ple_table: bfloat16 [262144, 256], P(('group', 'member')), may hold values from -0.375 to 0.375
- norm_gains: float32 [1, 3, 2048], replicated, may hold values from 0.1 to 1.9
- w_gate: bfloat16 [1, 2048, 8192], P(None, None, 'member'), may hold values from -0.125 to 0.125
- w_up: bfloat16 [1, 2048, 8192], P(None, None, 'member'), may hold values from -0.125 to 0.125
- w_down: bfloat16 [1, 8192, 2048], P(None, 'member'), may hold values from -0.0625 to 0.0625
- ple_gate: bfloat16 [1, 2048, 256], P(None, None, 'member'), may hold values from -0.125 to 0.125
- ple_proj: bfloat16 [1, 256, 2048], P(None, 'member'), may hold values from -0.375 to 0.375
Outputs:
- hidden_out: bfloat16 [12288, 2048], P('group')
Inputs may be any that keep to these rules, and one draw needn't show every extreme that they name: Within the 96 tokens of one device (aligned blocks of token_slab), no slab is named by more than 2 tokens. Each number appears once: slab s is stored in rows slab_owner[s] * 2048 to slab_owner[s] * 2048 + 2047 of ple_table.
All inputs are finite; a program needn't handle non-finite values.
Results may differ from a plain program's by a relative error of at most 0.0061.
Values may be sent and summed in bfloat16 or wider, within the bound.
A program may use at most 128 MiB of HBM per device.

v0:
```python
import jax
import jax.numpy as jnp
from jax import lax
from jax.sharding import PartitionSpec as P

PLE = 256
epsilon = 1e-06


def norm_rows(values, scales):
    return values * lax.rsqrt(jnp.mean(values * values, axis=-1, keepdims=True) + epsilon) * scales


def per_device(
    hidden,
    token_slab,
    token_row,
    slab_owner,
    ple_table,
    norm_gains,
    w_gate,
    w_up,
    w_down,
    ple_gate,
    ple_proj,
):
    members = lax.axis_size("member")
    devices = lax.axis_size("group") * members
    tokens_here = token_row.shape[0]
    slots = max(2, (2 * tokens_here + devices - 1) // devices)
    me = lax.axis_index("member")
    gate_full = lax.all_gather(ple_gate[0].T, "member", axis=0, tiled=True)
    proj_full = lax.all_gather(ple_proj[0], "member", axis=0, tiled=True)
    normed = norm_rows(hidden.astype(jnp.float32), norm_gains[0, 0]).astype(jnp.bfloat16)
    gate_part = jnp.dot(normed, w_gate[0], preferred_element_type=jnp.float32)
    up_part = jnp.dot(normed, w_up[0], preferred_element_type=jnp.float32)
    activated = (jax.nn.gelu(gate_part, approximate=True) * up_part).astype(jnp.bfloat16)
    partial = jnp.dot(activated, w_down[0], preferred_element_type=jnp.float32).astype(jnp.bfloat16)
    mlp_out = lax.psum_scatter(partial, "member", scatter_dimension=0, tiled=True).astype(
        jnp.float32
    )
    target = slab_owner[token_slab[:, 0]]
    order = jnp.arange(tokens_here, dtype=jnp.int32)
    earlier = (target[None, :] == target[:, None]) & (order[None, :] < order[:, None])
    slot_of = jnp.sum(earlier.astype(jnp.int32), axis=1)
    hit_map = (target[:, None, None] == jnp.arange(devices, dtype=jnp.int32)[None, :, None]) & (
        slot_of[:, None, None] == jnp.arange(slots, dtype=jnp.int32)[None, None, :]
    )
    requests = jnp.sum(jnp.where(hit_map, token_row[:, None, None] + 1, 0), axis=0)
    received = lax.all_to_all(
        requests, ("group", "member"), split_axis=0, concat_axis=0, tiled=True
    )
    flat_ids = received.reshape(-1) - 1
    one_hot = (
        flat_ids[:, None] == jnp.arange(ple_table.shape[0], dtype=jnp.int32)[None, :]
    ).astype(jnp.bfloat16)
    served = jnp.dot(one_hot, ple_table, preferred_element_type=jnp.float32).astype(jnp.bfloat16)
    served = served.reshape(devices, slots * ple_table.shape[1])
    returned = lax.all_to_all(served, ("group", "member"), split_axis=0, concat_axis=0, tiled=True)
    returned = returned.reshape(devices * slots, ple_table.shape[1])
    own_rows = jnp.dot(
        hit_map.reshape(tokens_here, devices * slots).astype(jnp.bfloat16),
        returned,
        preferred_element_type=jnp.float32,
    )
    mine = lax.dynamic_slice_in_dim(hidden, me * tokens_here, tokens_here, 0).astype(jnp.float32)
    current = mine + norm_rows(mlp_out, norm_gains[0, 1])
    current_b = current.astype(jnp.bfloat16)
    gate_out = lax.dot_general(
        current_b, gate_full, (((1,), (1,)), ((), ())), preferred_element_type=jnp.float32
    )
    ple_act = (jax.nn.gelu(gate_out, approximate=True) * (own_rows * PLE**0.5)).astype(jnp.bfloat16)
    ple_out = jnp.dot(ple_act, proj_full, preferred_element_type=jnp.float32)
    current = current + norm_rows(ple_out, norm_gains[0, 2])
    return lax.all_gather(current.astype(jnp.bfloat16), "member", axis=0, tiled=True)


def solution(mesh):
    return jax.shard_map(
        per_device,
        mesh=mesh,
        in_specs=(
            P("group", None),
            P(("group", "member"), None),
            P(("group", "member")),
            P(),
            P(("group", "member"), None),
            P(),
            P(None, None, "member"),
            P(None, None, "member"),
            P(None, "member", None),
            P(None, None, "member"),
            P(None, "member", None),
        ),
        out_specs=P("group", None),
        check_vma=False,
    )
```

profile of v0, /device:TPU:1, one launch (start us, length us, event | category | flops | bytes accessed | tf_op | source)
XLA Modules:
  0.0 283.0 jit_solution(1658720977791138758)
XLA Ops:
  6.5 0.0 copy-start
  6.5 0.0 copy-start.4
  6.5 0.0 reduce-scatter.2.cloned.1.call-start
  6.5 0.0 copy-start.2
  6.5 4.2 %fusion = f32[1536]{0:T(1024)S(1)} fusion(bf16[1536,2048]{1,0:T(8,128)(2,1)} %param.11), kind=kLoop, calls=%fused_computation.3 | loop fusion | flops 9435648 | bytes 6297600 | tf_op jit(solution)/shard_map/reduce_sum | solution.py:11
  10.8 0.0 copy-done.4
  10.8 0.5 copy-done.2
  11.3 6.8 %fusion.13 = f32[1536,512]{1,0:T(8,128)} fusion(bf16[1,2048,512]{2,1,0:T(8,128)(2,1)} %param.17, bf16[1536,2048]{1,0:T(8,128)(2,1)S(1)} %copy-done.2, f32[2048]{0:T(1024)S(1)} %bitcast.36, f32[1536]{0:T(1024)S(1)} %add_rsqrt_fusion), kind=kOutput, calls=%fused_computation.19 | convolution fusion | flops 3233808384 | bytes 11548672 | tf_op jit(solution)/shard_map/dot_general | solution.py:35
  18.1 0.0 copy-done
  18.1 12.4 %convolution_convert_fusion = bf16[1536,2048]{1,0:T(8,128)(2,1)} fusion(bf16[1,512,2048]{2,1,0:T(8,128)(2,1)S(1)} %copy-done, f32[1536,512]{1,0:T(8,128)} %fusion.13, bf16[1,2048,512]{2,1,0:T(8,128)(2,1)} %param.18, bf16[1536,2048]{1,0:T(8,128)(2,1)} %param.11, f32[2048]{0:T(1024)S(1)} %bitcast.37, f32[1536]{0:T(1024)S(1)} %add_rsqrt_fusion), kind=kOutput, calls=%fused_computation.6 | convolution fusion | flops 6466043904 | bytes 19937280 | tf_op jit(solution)/shard_map/dot_general | solution.py:38
  30.5 0.0 copy-start.6
  30.5 0.0 copy-start.7
  30.5 0.0 copy-start.1
  30.5 0.0 reduce-scatter.2.cloned.1.call-update
  30.5 0.0 all-gather.5.cloned.1.call-start
  30.6 0.7 all-gather.5.cloned.1.call-update
  31.3 0.0 all-gather.9.cloned.1.call-start
  31.3 0.7 all-gather.9.cloned.1.call-update
  32.0 0.0 copy-done.6
  32.0 0.0 copy-done.7
  32.1 0.0 copy-done.1
  32.1 1.2 gather_fusion
  33.3 0.2 convert_reduce_fusion
  33.5 2.2 select_reduce_fusion
  35.8 21.2 %all_to_all.19 = s32[128,1,2]{2,1,0:T(1,128)S(1)} all-to-all(s32[128,1,2]{2,1,0:T(1,128)S(1)} %bitcast.31), channel_id=1, replica_groups=mesh['group'=8,'member'=16] {'group','member'}, dimensions={0} | all-to-all | bytes 2048 | tf_op jit(solution)/shard_map/all_to_all | solution.py:50
  56.9 0.2 add_reduce_fusion
  57.1 0.1 sub.7
  57.2 1.7 fusion.22
  59.0 0.1 all_to_all.16
  59.0 0.6 broadcast.109
  59.6 1.4 reduce.5
  61.0 0.7 reshape.127
  61.7 4.4 %all-to-all-start.1 = ((bf16[128,2,256]{2,1,0:T(2,128)(2,1)}), bf16[128,2,256]{2,1,0:T(2,128)(2,1)S(1)}, u32[]{:S(2)}, u32[]{:S(2)}) async-start(bf16[128,2,256]{2,1,0:T(2,128)(2,1)} %reshape.127), calls=%async_computation.2 | async-start | bytes 262144 | tf_op jit(solution)/shard_map/all_to_all | solution.py:59
  66.1 0.0 all-gather.7.cloned.1.call-start
  66.1 0.1 and.31
  66.2 10.9 %all-to-all-done.1 = bf16[128,2,256]{2,1,0:T(2,128)(2,1)S(1)} async-done(((bf16[128,2,256]{2,1,0:T(2,128)(2,1)}), bf16[128,2,256]{2,1,0:T(2,128)(2,1)S(1)}, u32[]{:S(2)}, u32[]{:S(2)}) %all-to-all-start.1) | async-done | bytes 131104 | tf_op jit(solution)/shard_map/all_to_all | solution.py:59
  77.1 0.1 reshape.128
  77.2 0.8 reduce.1
  78.1 36.8 %reduce-scatter.2.cloned.1.call-done = bf16[96,2048]{1,0:T(8,128)(2,1)} async-done(((bf16[1536,2048]{1,0:T(8,128)(2,1)}), bf16[96,2048]{1,0:T(8,128)(2,1)}) %reduce-scatter.2.cloned.1.call-update) | async-done | bytes 393232 | tf_op jit(solution)/shard_map/reduce_scatter | solution.py:39
  114.9 0.0 copy-start.3
  114.9 1.2 fusion.28
  116.2 0.0 copy-start.5
  116.2 42.5 %all-gather.5.cloned.1.call-done = bf16[256,2048]{1,0:T(8,128)(2,1)} async-done(((bf16[16,2048]{1,0:T(8,128)(2,1)}), bf16[256,2048]{1,0:T(8,128)(2,1)}) %all-gather.5.cloned.1.call-update) | async-done | bytes 1048592 | tf_op jit(solution)/shard_map/all_gather | solution.py:32
  158.7 2.0 fusion.43
  160.6 0.0 copy-done.5
  160.6 42.0 %all-gather.9.cloned.1.call-done = bf16[1,256,2048]{2,1,0:T(8,128)(2,1)} async-done(((bf16[1,16,2048]{2,1,0:T(8,128)(2,1)}), bf16[1,256,2048]{2,1,0:T(8,128)(2,1)}) %all-gather.9.cloned.1.call-update) | async-done | bytes 1048592 | tf_op jit(solution)/shard_map/all_gather | solution.py:33
  202.7 2.3 multiply_reduce_fusion
  205.0 0.7 add_rsqrt_fusion.1
  205.7 0.0 copy-done.3
  205.7 2.1 add_convert_fusion
  207.8 0.0 all-gather.7.cloned.1.call-update
  207.8 62.1 %all-gather.7.cloned.1.call-done = bf16[1536,2048]{1,0:T(8,128)(2,1)} async-done(((bf16[96,2048]{1,0:T(8,128)(2,1)}), bf16[1536,2048]{1,0:T(8,128)(2,1)}) %all-gather.7.cloned.1.call-update) | async-done | bytes 6291472 | tf_op jit(solution)/shard_map/all_gather | solution.py:75
  269.9 6.6 %copy.17 = bf16[1536,2048]{1,0:T(8,128)(2,1)} copy(bf16[1536,2048]{1,0:T(8,128)(2,1)} %all-gather.7.cloned.1.call-done) | data formatting | bytes 12582912
  (9 shorter events, 0.1 us)
Async XLA Ops:
  6.5 11.6 %copy-start = (bf16[1,512,2048]{2,1,0:T(8,128)(2,1)S(1)}, bf16[1,512,2048]{2,1,0:T(8,128)(2,1)}, u32[]{:S(2)}) copy-start(bf16[1,512,2048]{2,1,0:T(8,128)(2,1)} %param.19) | copy-start | bytes 6291460
  6.5 4.3 %copy-start.4 = (f32[1,3,2048]{2,0,1:T(1,128)S(1)}, f32[1,3,2048]{2,0,1:T(1,128)}, u32[]{:S(2)}) copy-start(f32[1,3,2048]{2,0,1:T(1,128)} %param.16) | copy-start | bytes 73732
  6.5 108.4 %reduce-scatter.2.cloned.1.call-start = ((), (), s32[]{:S(2)}) async-start(), calls=%async_computation.3 | async-start | bytes 6684672 | tf_op jit(solution)/shard_map/reduce_scatter | solution.py:39
  6.5 4.8 %copy-start.2 = (bf16[1536,2048]{1,0:T(8,128)(2,1)S(1)}, bf16[1536,2048]{1,0:T(8,128)(2,1)}, u32[]{:S(2)}) copy-start(bf16[1536,2048]{1,0:T(8,128)(2,1)} %param.11) | copy-start | bytes 18874372
  30.5 1.5 copy-start.6
  30.5 1.5 copy-start.7
  30.5 1.6 copy-start.1
  30.5 128.1 %all-gather.5.cloned.1.call-start = ((), (), s32[]{:S(2)}) async-start(), calls=%async_computation.4 | async-start | bytes 1114112 | tf_op jit(solution)/shard_map/all_gather | solution.py:32
  31.3 171.4 %all-gather.9.cloned.1.call-start = ((), (), s32[]{:S(2)}) async-start(), calls=%async_computation.6 | async-start | bytes 1114112 | tf_op jit(solution)/shard_map/all_gather | solution.py:33
  61.7 15.5 %all-to-all-start.1 = ((bf16[128,2,256]{2,1,0:T(2,128)(2,1)}), bf16[128,2,256]{2,1,0:T(2,128)(2,1)S(1)}, u32[]{:S(2)}, u32[]{:S(2)}) async-start(bf16[128,2,256]{2,1,0:T(2,128)(2,1)} %reshape.127), calls=%async_computation.2 | async-start | bytes 262144 | tf_op jit(solution)/shard_map/all_to_all | solution.py:59
  66.1 203.8 %all-gather.7.cloned.1.call-start = ((), (), s32[]{:S(2)}) async-start(), calls=%async_computation.5 | async-start | bytes 6684672 | tf_op jit(solution)/shard_map/all_gather | solution.py:75
  114.9 90.8 %copy-start.3 = (bf16[96,2048]{1,0:T(8,128)(2,1)S(1)}, bf16[96,2048]{1,0:T(8,128)(2,1)}, u32[]{:S(2)}) copy-start(bf16[96,2048]{1,0:T(8,128)(2,1)} %reduce-scatter.2.cloned.1.call-done) | copy-start | bytes 1179652
  116.2 44.5 %copy-start.5 = (f32[96]{0:T(128)}, f32[96]{0:T(128)S(1)}, u32[]{:S(2)}) copy-start(f32[96]{0:T(128)S(1)} %add_rsqrt_fusion.2) | copy-start | bytes 1156
Sparse Core Ops, SparseCore 0:
  30.6 84.2 reduce-scatter.1
  117.0 41.5 all-gather.4
  160.8 41.8 all-gather.8
  207.9 61.9 all-gather.6
where the time goes:
time: 283 us
  waiting for transfers between devices  196 us (69%)
  matrix products  25.2 us (9%)
  blocking collectives  21.2 us (7%)
  between operations  13.3 us (5%)
  other arithmetic  13 us (5%)
  local copies, waits for them, and re-layouts  10 us (4%)
  starting transfers between devices  4.54 us (2%)
    all_gather x1, waiting for transfers between devices, per_device(): lax.all_gather(current.astype(jnp.bfloat16), 'member', axis=0, tiled=True)  62.1 us
    all_gather x1, waiting for transfers between devices, per_device(): gate_full = lax.all_gather(ple_gate[0].T, 'member', axis=0, tiled=True)  42.5 us
    all_gather x1, waiting for transfers between devices, per_device(): proj_full = lax.all_gather(ple_proj[0], 'member', axis=0, tiled=True)  42 us
    reduce_scatter x1, waiting for transfers between devices, per_device(): lax.psum_scatter(partial, 'member', scatter_dimension=0, tiled=True)  36.8 us
    all_to_all x1, blocking collectives, per_device(): lax.all_to_all(requests, ('group', 'member'), split_axis=0, concat_axis=0...  21.2 us
    dot_general x1, matrix products, per_device(): jnp.dot(activated, w_down[0], preferred_element_type=jnp.float32)  12.4 us
    all_to_all x1, waiting for transfers between devices, per_device(): lax.all_to_all(served, ('group', 'member'), split_axis=0, concat_axis=0,...  10.9 us
    unnamed x19, local copies, waits for them, and re-layouts  7.92 us
  transfers between devices with their start and end apart: 5, of which 5 were waited for; matrix products, arithmetic and copies ran while one was open for 4% of the time, Pallas kernels for 0%

commit v1 on v0

--- a/solution.py
+++ b/solution.py
@@ -29,7 +29,9 @@
     tokens_here = token_row.shape[0]
     slots = max(2, (2 * tokens_here + devices - 1) // devices)
     me = lax.axis_index("member")
-    gate_full = lax.all_gather(ple_gate[0].T, "member", axis=0, tiled=True)
+    gate_full = jnp.concatenate(
+        lax.all_to_all(jnp.stack([ple_gate[0].T] * lax.axis_size("member")), "member", 0, 0), axis=0
+    )
     proj_full = lax.all_gather(ple_proj[0], "member", axis=0, tiled=True)
     normed = norm_rows(hidden.astype(jnp.float32), norm_gains[0, 0]).astype(jnp.bfloat16)
     gate_part = jnp.dot(normed, w_gate[0], preferred_element_type=jnp.float32)

time: 283 us -> 246 us (0.87)
  waiting for transfers between devices: 196 us -> 142 us
  blocking collectives: 21.2 us -> 35.7 us
    all_gather x1 -> x0, waiting for transfers between devices: 42.5 us -> none  [per_device(): gate_full = lax.all_gather(ple_gate[0].T, 'member', axis=0, tiled=True)]
    all_to_all x0 -> x1, blocking collectives: none -> 14.6 us  [per_device(): lax.all_to_all(served, ('group', 'member'), split_axis=0, concat_axis=0,...]
    all_to_all x1, waiting for transfers between devices: 10.9 us -> 0.01 us  [per_device(): lax.all_to_all(jnp.stack([ple_gate[0].T] * lax.axis_size('member')), 'mem...]
  transfers between devices with their start and end apart: 5 -> 4, of which waited for: 5 -> 3; matrix products, arithmetic and copies ran while one was open for 4% -> 7% of each run, Pallas kernels for 0% -> 0%
where the time goes in v1:
time: 246 us
  waiting for transfers between devices  142 us (58%)
  blocking collectives  35.7 us (15%)
  matrix products  25.1 us (10%)
  other arithmetic  13.4 us (5%)
  between operations  13.3 us (5%)
  local copies, waits for them, and re-layouts  12.7 us (5%)
  starting transfers between devices  3.74 us (2%)
    all_gather x1, waiting for transfers between devices, per_device(): lax.all_gather(current.astype(jnp.bfloat16), 'member', axis=0, tiled=True)  62.1 us
    all_gather x1, waiting for transfers between devices, per_device(): proj_full = lax.all_gather(ple_proj[0], 'member', axis=0, tiled=True)  39.7 us
    reduce_scatter x1, waiting for transfers between devices, per_device(): lax.psum_scatter(partial, 'member', scatter_dimension=0, tiled=True)  39.6 us
    all_to_all x1, blocking collectives, per_device(): lax.all_to_all(requests, ('group', 'member'), split_axis=0, concat_axis=0...  21.1 us
    all_to_all x1, blocking collectives, per_device(): lax.all_to_all(served, ('group', 'member'), split_axis=0, concat_axis=0,...  14.6 us
    dot_general x1, matrix products, per_device(): jnp.dot(activated, w_down[0], preferred_element_type=jnp.float32)  12.4 us
    unnamed x19, local copies, waits for them, and re-layouts  7.27 us
    dot_general x1, matrix products, per_device(): gate_part = jnp.dot(normed, w_gate[0], preferred_element_type=jnp.float32)  6.81 us
  transfers between devices with their start and end apart: 4, of which 3 were waited for; matrix products, arithmetic and copies ran while one was open for 7% of the time, Pallas kernels for 0%

profile of v1, /device:TPU:1, one launch (start us, length us, event | category | flops | bytes accessed | tf_op | source)
XLA Modules:
  0.0 246.0 jit_solution(4342978858987168150)
XLA Ops:
  6.5 0.0 copy-start
  6.5 0.0 copy-start.5
  6.5 0.0 reduce-scatter.2.cloned.1.call-start
  6.5 0.0 copy-start.2
  6.5 4.2 %fusion = f32[1536]{0:T(1024)S(1)} fusion(bf16[1536,2048]{1,0:T(8,128)(2,1)} %param.11), kind=kLoop, calls=%fused_computation.3 | loop fusion | flops 9435648 | bytes 6297600 | tf_op jit(solution)/shard_map/reduce_sum | solution.py:11
  10.8 0.0 copy-done.5
  10.8 0.5 copy-done.2
  11.3 6.8 %fusion.13 = f32[1536,512]{1,0:T(8,128)} fusion(bf16[1,2048,512]{2,1,0:T(8,128)(2,1)} %param.17, bf16[1536,2048]{1,0:T(8,128)(2,1)S(1)} %copy-done.2, f32[2048]{0:T(1024)S(1)} %bitcast.38, f32[1536]{0:T(1024)S(1)} %add_rsqrt_fusion), kind=kOutput, calls=%fused_computation.19 | convolution fusion | flops 3233808384 | bytes 11548672 | tf_op jit(solution)/shard_map/dot_general | solution.py:37
  18.1 0.0 copy-done
  18.1 12.4 %convolution_convert_fusion = bf16[1536,2048]{1,0:T(8,128)(2,1)} fusion(bf16[1,512,2048]{2,1,0:T(8,128)(2,1)S(1)} %copy-done, f32[1536,512]{1,0:T(8,128)} %fusion.13, bf16[1,2048,512]{2,1,0:T(8,128)(2,1)} %param.18, bf16[1536,2048]{1,0:T(8,128)(2,1)} %param.11, f32[2048]{0:T(1024)S(1)} %bitcast.39, f32[1536]{0:T(1024)S(1)} %add_rsqrt_fusion), kind=kOutput, calls=%fused_computation.6 | convolution fusion | flops 6466043904 | bytes 19937280 | tf_op jit(solution)/shard_map/dot_general | solution.py:40
  30.5 0.0 copy-start.6
  30.5 0.0 copy-start.1
  30.5 0.0 copy-start.7
  30.5 0.0 reduce-scatter.2.cloned.1.call-update
  30.5 0.0 copy-start.4
  30.5 0.0 all-gather.6.cloned.1.call-start
  30.6 0.7 all-gather.6.cloned.1.call-update
  31.3 0.0 copy-done.6
  31.3 0.0 copy-done.1
  31.3 1.2 gather_fusion
  32.6 0.2 convert_reduce_fusion
  32.8 0.0 copy-done.7
  32.8 2.7 %select_reduce_fusion = (s32[128,2]{1,0:T(8,128)S(1)}, pred[96,128,2]{0,2,1:T(4,128)(4,1)}) fusion(s32[96]{0:T(128)S(1)} %broadcast_add_fusion, pred[96,2]{0,1:T(4,128)(4,1)S(1)} %iota_compare_fusion.6, pred[96,128]{0,1:T(8,128)(4,1)S(1)} %iota_compare_fusion.4), kind=kLoop, calls=%fused_computation.43 | loop fusion | flops 73472 | bytes 38464 | tf_op jit(solution)/shard_map/reduce_sum | solution.py:51
  35.5 21.1 %all_to_all.24 = s32[128,1,2]{2,1,0:T(1,128)S(1)} all-to-all(s32[128,1,2]{2,1,0:T(1,128)S(1)} %bitcast.33), channel_id=1, replica_groups=mesh['group'=8,'member'=16] {'group','member'}, dimensions={0} | all-to-all | bytes 2048 | tf_op jit(solution)/shard_map/all_to_all | solution.py:52
  56.5 0.2 add_reduce_fusion
  56.7 0.1 sub.7
  56.9 1.7 fusion.22
  58.6 0.1 all_to_all.20
  58.7 0.6 broadcast.111
  59.3 1.4 reduce.5
  60.7 14.6 %all_to_all.25 = bf16[128,2,256]{2,1,0:T(2,128)(2,1)S(1)} all-to-all(bf16[128,2,256]{2,1,0:T(2,128)(2,1)S(1)} %reshape.133), channel_id=1, replica_groups=mesh['group'=8,'member'=16] {'group','member'}, dimensions={0} | all-to-all | bytes 262144 | tf_op jit(solution)/shard_map/all_to_all | solution.py:61
  75.4 0.0 copy-done.4
  75.4 1.2 stack.2
  76.5 3.7 %all-to-all-start = ((bf16[16,16,2048]{2,1,0:T(8,128)(2,1)}), bf16[16,16,2048]{2,1,0:T(8,128)(2,1)S(1)}, u32[]{:S(2)}, u32[]{:S(2)}) async-start(bf16[16,16,2048]{2,1,0:T(8,128)(2,1)} %stack.2), calls=%async_computation.1 | async-start | bytes 2097152 | tf_op jit(solution)/shard_map/all_to_all | solution.py:33
  80.2 0.0 all-gather.4.cloned.1.call-start
  80.2 1.5 and.31
  81.8 0.1 reshape.134
  81.9 0.8 reduce.1
  82.6 0.7 reshape.115
  83.3 39.6 %reduce-scatter.2.cloned.1.call-done = bf16[96,2048]{1,0:T(8,128)(2,1)} async-done(((bf16[1536,2048]{1,0:T(8,128)(2,1)}), bf16[96,2048]{1,0:T(8,128)(2,1)}) %reduce-scatter.2.cloned.1.call-update) | async-done | bytes 393232 | tf_op jit(solution)/shard_map/reduce_scatter | solution.py:41
  122.9 0.0 copy-start.3
  122.9 1.2 fusion.28
  124.2 0.5 add_rsqrt_fusion.2
  124.7 0.0 all-to-all-done
  124.7 2.3 fusion.43
  127.0 39.7 %all-gather.6.cloned.1.call-done = bf16[1,256,2048]{2,1,0:T(8,128)(2,1)} async-done(((bf16[1,16,2048]{2,1,0:T(8,128)(2,1)}), bf16[1,256,2048]{2,1,0:T(8,128)(2,1)}) %all-gather.6.cloned.1.call-update) | async-done | bytes 1048592 | tf_op jit(solution)/shard_map/all_gather | solution.py:35
  166.7 2.0 multiply_reduce_fusion
  168.7 0.0 copy-done.3
  168.7 2.1 add_convert_fusion
  170.8 0.0 all-gather.4.cloned.1.call-update
  170.8 62.1 %all-gather.4.cloned.1.call-done = bf16[1536,2048]{1,0:T(8,128)(2,1)} async-done(((bf16[96,2048]{1,0:T(8,128)(2,1)}), bf16[1536,2048]{1,0:T(8,128)(2,1)}) %all-gather.4.cloned.1.call-update) | async-done | bytes 6291472 | tf_op jit(solution)/shard_map/all_gather | solution.py:77
  232.9 6.6 %copy.17 = bf16[1536,2048]{1,0:T(8,128)(2,1)} copy(bf16[1536,2048]{1,0:T(8,128)(2,1)} %all-gather.4.cloned.1.call-done) | data formatting | bytes 12582912
  (9 shorter events, 0.1 us)
Async XLA Ops:
  6.5 11.6 %copy-start = (bf16[1,512,2048]{2,1,0:T(8,128)(2,1)S(1)}, bf16[1,512,2048]{2,1,0:T(8,128)(2,1)}, u32[]{:S(2)}) copy-start(bf16[1,512,2048]{2,1,0:T(8,128)(2,1)} %param.19) | copy-start | bytes 6291460
  6.5 4.3 %copy-start.5 = (f32[1,3,2048]{2,0,1:T(1,128)S(1)}, f32[1,3,2048]{2,0,1:T(1,128)}, u32[]{:S(2)}) copy-start(f32[1,3,2048]{2,0,1:T(1,128)} %param.16) | copy-start | bytes 73732
  6.5 116.4 %reduce-scatter.2.cloned.1.call-start = ((), (), s32[]{:S(2)}) async-start(), calls=%async_computation.4 | async-start | bytes 6684672 | tf_op jit(solution)/shard_map/reduce_scatter | solution.py:41
  6.5 4.8 %copy-start.2 = (bf16[1536,2048]{1,0:T(8,128)(2,1)S(1)}, bf16[1536,2048]{1,0:T(8,128)(2,1)}, u32[]{:S(2)}) copy-start(bf16[1536,2048]{1,0:T(8,128)(2,1)} %param.11) | copy-start | bytes 18874372
  30.5 0.8 copy-start.6
  30.5 0.8 copy-start.1
  30.5 2.3 copy-start.7
  30.5 44.9 %copy-start.4 = (bf16[1,2048,16]{1,2,0:T(8,128)(2,1)S(1)}, bf16[1,2048,16]{1,2,0:T(8,128)(2,1)}, u32[]{:S(2)}) copy-start(bf16[1,2048,16]{1,2,0:T(8,128)(2,1)} %param.20) | copy-start | bytes 196612
  30.5 136.2 %all-gather.6.cloned.1.call-start = ((), (), s32[]{:S(2)}) async-start(), calls=%async_computation.6 | async-start | bytes 1114112 | tf_op jit(solution)/shard_map/all_gather | solution.py:35
  76.5 48.2 %all-to-all-start = ((bf16[16,16,2048]{2,1,0:T(8,128)(2,1)}), bf16[16,16,2048]{2,1,0:T(8,128)(2,1)S(1)}, u32[]{:S(2)}, u32[]{:S(2)}) async-start(bf16[16,16,2048]{2,1,0:T(8,128)(2,1)} %stack.2), calls=%async_computation.1 | async-start | bytes 2097152 | tf_op jit(solution)/shard_map/all_to_all | solution.py:33
  80.2 152.7 %all-gather.4.cloned.1.call-start = ((), (), s32[]{:S(2)}) async-start(), calls=%async_computation.5 | async-start | bytes 6684672 | tf_op jit(solution)/shard_map/all_gather | solution.py:77
  122.9 45.7 %copy-start.3 = (bf16[96,2048]{1,0:T(8,128)(2,1)S(1)}, bf16[96,2048]{1,0:T(8,128)(2,1)}, u32[]{:S(2)}) copy-start(bf16[96,2048]{1,0:T(8,128)(2,1)} %reduce-scatter.2.cloned.1.call-done) | copy-start | bytes 1179652
Sparse Core Ops, SparseCore 0:
  30.6 92.2 reduce-scatter.1
  125.1 41.5 all-gather.5
  170.9 61.9 all-gather.3
